TPU v7x, 32 devices: a whole 2x2x4 slice. The times are simulated.
32 devices in a mesh: dp: 4 (over z), expert: 4 (over y, core), loop: 2 (over x).
Axes of the slice: x: 2, y: 2, z: 4, core: 2. Of those that a mesh axis runs over, the one named last changes fastest.
Arguments:
- x_send: bfloat16 [512, 4096], P(('dp', 'expert', 'loop')), may hold values from -6 to 6
- cot_send: bfloat16 [512, 4096], P(('dp', 'expert', 'loop')), may hold values from -6 to 6
- counts: int32 [32, 4], P(('dp', 'expert', 'loop')), may hold values from 0 to 4, as said below
- w_gate: bfloat16 [4, 4096, 768], P('expert', None, 'loop'), may hold values from -0.09375 to 0.09375
- w_up: bfloat16 [4, 4096, 768], P('expert', None, 'loop'), may hold values from -0.09375 to 0.09375
- w_down: bfloat16 [4, 4096, 768], P('expert', None, 'loop'), may hold values from -0.21875 to 0.21875
Outputs:
- grad_rows: bfloat16 [512, 4096], P(('dp', 'expert', 'loop'))
- grad_down: float32 [4, 4096, 768], P('expert', 'dp', 'loop')
Inputs may be any that keep to these rules, and one draw needn't show every extreme that they name: counts[s, e] is how many of the 4 slots of device s for owner e hold rows, filled from slot 0; in each group of 8 consecutive devices one owner, drawn anew, receives 4 rows from every device, and every other owner at most 2 from each device.
All inputs are finite; a program needn't handle non-finite values.
Results may differ from a plain program's by a relative error of at most 0.0095.
Values may be sent and summed in bfloat16 or wider, within the bound.
No kernel may reach another device: no remote copies, remote signals or barrier semaphores. Data moves between devices by JAX's collectives and lax.ppermute only.
A program may use at most 64 MiB of HBM per device.

v0:
```python
import jax
import jax.numpy as jnp
from jax import lax
from jax.sharding import PartitionSpec as P


def local(x_send, cot_send, counts, w_gate, w_up, w_down):
    owner_count = counts.shape[1]
    capacity = x_send.shape[0] // owner_count
    live_slot = (jnp.arange(capacity, dtype=jnp.int32)[None, :] < counts[0][:, None]).reshape(
        owner_count * capacity, 1
    )
    zero_value = jnp.zeros((), jnp.bfloat16)
    inputs = jnp.where(live_slot, x_send, zero_value)
    cotans = jnp.where(live_slot, cot_send, zero_value)
    arrived, arrived_cot = (
        lax.all_to_all(inputs, "expert", split_axis=0, concat_axis=0, tiled=True),
        lax.all_to_all(cotans, "expert", split_axis=0, concat_axis=0, tiled=True),
    )
    gathered, gathered_cot = (
        lax.all_gather(arrived, "loop", axis=0, tiled=True),
        lax.all_gather(arrived_cot, "loop", axis=0, tiled=True),
    )
    gate_local = w_gate[0]
    up_local = w_up[0]
    down_local = w_down[0]
    gate_pre = jnp.dot(gathered, gate_local, preferred_element_type=jnp.float32)
    up_proj = jnp.dot(gathered, up_local, preferred_element_type=jnp.float32)
    sigmoid_gate = jax.nn.sigmoid(gate_pre)
    active = gate_pre * sigmoid_gate
    hidden = (active * up_proj).astype(jnp.bfloat16)
    grad_hidden = jnp.dot(gathered_cot, down_local, preferred_element_type=jnp.float32)
    grad_gate = (
        grad_hidden * up_proj * sigmoid_gate * (1.0 + gate_pre * (1.0 - sigmoid_gate))
    ).astype(jnp.bfloat16)
    grad_upp = (grad_hidden * active).astype(jnp.bfloat16)
    contract_last = (((1,), (1,)), ((), ()))
    contract_first = (((0,), (0,)), ((), ()))
    partial_value = lax.dot_general(
        grad_gate, gate_local, contract_last, preferred_element_type=jnp.float32
    )
    partial_value = partial_value + lax.dot_general(
        grad_upp, up_local, contract_last, preferred_element_type=jnp.float32
    )
    summed = lax.psum_scatter(
        lax.optimization_barrier(partial_value.astype(jnp.bfloat16))
        .astype(jnp.float32)
        .astype(jnp.bfloat16),
        "loop",
        scatter_dimension=0,
        tiled=True,
    )
    grad_rows = lax.all_to_all(summed, "expert", split_axis=0, concat_axis=0, tiled=True)
    column_part = lax.all_to_all(gathered_cot, "dp", split_axis=1, concat_axis=0, tiled=True)
    hidden_all = lax.all_gather(hidden, "dp", axis=0, tiled=True)
    result = lax.dot_general(
        column_part, hidden_all, contract_first, preferred_element_type=jnp.float32
    )
    grad_down = result[None]
    return (grad_rows, grad_down)


def solution(mesh):
    in_specs = (
        P(("dp", "expert", "loop"), None),
        P(("dp", "expert", "loop"), None),
        P(("dp", "expert", "loop"), None),
        P("expert", None, "loop"),
        P("expert", None, "loop"),
        P("expert", None, "loop"),
    )
    out_specs = (P(("dp", "expert", "loop"), None), P("expert", "dp", "loop"))
    return jax.shard_map(local, mesh=mesh, in_specs=in_specs, out_specs=out_specs, check_vma=False)
```

profile of v0, /device:TPU:0, one launch (start us, length us, event | category | flops | bytes accessed | tf_op | source)
XLA Modules:
  0.0 81.4 jit_solution(18439740056307525910)
XLA Ops:
  7.2 0.0 copy-start
  7.2 0.9 %iota_compare_fusion = pred[4,4]{1,0:T(4,128)(4,1)S(1)} fusion(s32[4]{0:T(128)} %bitcast.33), kind=kLoop, calls=%fused_computation.21 | loop fusion | flops 16 | bytes 32 | tf_op jit(solution)/shard_map/lt | solution.py:10
  8.1 0.1 lt.26
  8.1 1.1 %broadcast_select_fusion.1 = (bf16[16,4096]{1,0:T(8,128)(2,1)S(1)}, bf16[16,4096]{1,0:T(8,128)(2,1)S(1)}) fusion(bf16[16,4096]{1,0:T(8,128)(2,1)} %param.7, pred[16]{0:T(512)(128)(4,1)S(1)} %lt.26, bf16[16,4096]{1,0:T(8,128)(2,1)} %param.6), kind=kLoop, calls=%fused_computation.14 | loop fusion | flops 131072 | bytes 524304 | tf_op jit(solution)/shard_map/jit(_where)/select_n | solution.py:15
  9.2 0.7 all_to_all.38
  9.9 4.3 %all-to-all-start = ((bf16[4,4,4096]{2,1,0:T(4,128)(2,1)}), bf16[4,4,4096]{2,1,0:T(4,128)(2,1)S(1)}, u32[]{:S(2)}, u32[]{:S(2)}) async-start(bf16[4,4,4096]{2,1,0:T(4,128)(2,1)} %all_to_all.38), calls=%async_computation | async-start | bytes 262144 | tf_op jit(solution)/shard_map/all_to_all | solution.py:18
  14.2 0.7 all_to_all.41
  14.9 3.9 %all-to-all-done = bf16[4,4,4096]{2,1,0:T(4,128)(2,1)S(1)} async-done(((bf16[4,4,4096]{2,1,0:T(4,128)(2,1)}), bf16[4,4,4096]{2,1,0:T(4,128)(2,1)S(1)}, u32[]{:S(2)}, u32[]{:S(2)}) %all-to-all-start) | async-done | bytes 131104 | tf_op jit(solution)/shard_map/all_to_all | solution.py:18
  18.8 4.0 %all-to-all-start.1 = ((bf16[4,4,4096]{2,1,0:T(4,128)(2,1)}), bf16[4,4,4096]{2,1,0:T(4,128)(2,1)}, u32[]{:S(2)}, u32[]{:S(2)}) async-start(bf16[4,4,4096]{2,1,0:T(4,128)(2,1)} %all_to_all.41), calls=%async_computation.1 | async-start | bytes 262144 | tf_op jit(solution)/shard_map/all_to_all | solution.py:17
  22.7 0.0 reduce-scatter.2.cloned.1.call-start
  22.8 6.7 %all_gather.9 = bf16[32,4096]{1,0:T(8,128)(2,1)S(1)} all-gather(bf16[16,4096]{1,0:T(8,128)(2,1)S(1)} %all_to_all.40), channel_id=1, replica_groups=mesh['dp'=4,'expert'=4,'loop'=2] {'loop'}, dimensions={0}, use_global_device_ids=true | all-gather | bytes 393216 | tf_op jit(solution)/shard_map/all_gather | solution.py:22
  29.6 0.0 all-to-all-done.1
  29.6 0.9 %all_to_all.43 = bf16[16,4096]{1,0:T(8,128)(2,1)S(1)} reshape(bf16[4,4,4096]{2,1,0:T(4,128)(2,1)} %all-to-all-done.1) | data formatting | bytes 262144 | tf_op jit(solution)/shard_map/all_to_all | solution.py:17
  30.5 0.0 copy-start.1
  30.5 6.0 %all_gather.10 = bf16[32,4096]{1,0:T(8,128)(2,1)S(1)} all-gather(bf16[16,4096]{1,0:T(8,128)(2,1)S(1)} %all_to_all.43), channel_id=1, replica_groups=mesh['dp'=4,'expert'=4,'loop'=2] {'loop'}, dimensions={0}, use_global_device_ids=true | all-gather | bytes 393216 | tf_op jit(solution)/shard_map/all_gather | solution.py:21
  36.5 2.4 %fusion.8 = f32[32,384]{1,0:T(8,128)S(1)} fusion(bf16[32,4096]{1,0:T(8,128)(2,1)S(1)} %all_gather.9, bf16[1,4096,384]{2,1,0:T(8,128)(2,1)} %param.11), kind=kOutput, calls=%fused_computation.9 | convolution fusion | flops 100663296 | bytes 3457024 | tf_op jit(solution)/shard_map/dot_general | solution.py:32
  39.0 0.0 copy-done.1
  39.0 0.5 fusion.3
  39.5 0.0 copy-done
  39.5 0.6 multiply_convert_fusion
  40.1 1.1 %fusion.1 = f32[32,4096]{1,0:T(8,128)S(1)} fusion(bf16[1,4096,384]{2,1,0:T(8,128)(2,1)S(1)} %copy-done.1, f32[32,384]{1,0:T(8,128)S(1)} %fusion.3, f32[32,384]{1,0:T(8,128)S(1)} %fusion.8, f32[32,384]{1,0:T(8,128)S(1)} %get-tuple-element.5), kind=kOutput, calls=%fused_computation.2 | convolution fusion | flops 100786176 | bytes 3817472 | tf_op jit(solution)/shard_map/dot_general | solution.py:39
  41.2 1.8 %fusion = bf16[32,4096]{1,0:T(8,128)(2,1)} fusion(f32[32,4096]{1,0:T(8,128)S(1)} %fusion.1, bf16[1,4096,384]{2,1,0:T(8,128)(2,1)S(1)} %copy-done, f32[32,384]{1,0:T(8,128)S(1)} %fusion.8, f32[32,384]{1,0:T(8,128)S(1)} %fusion.3), kind=kOutput, calls=%fused_computation.1 | convolution fusion | flops 100999168 | bytes 4030464 | tf_op jit(solution)/shard_map/dot_general | solution.py:42
  42.9 0.0 reduce-scatter.2.cloned.1.call-update
  43.0 0.7 copy.12
  43.7 4.9 %all-to-all-start.3 = ((bf16[32,4,1024]{2,0,1:T(8,128)(2,1)}), bf16[32,4,1024]{2,0,1:T(8,128)(2,1)S(1)}, u32[]{:S(2)}, u32[]{:S(2)}) async-start(bf16[32,4,1024]{2,0,1:T(8,128)(2,1)} %bitcast.31), calls=%async_computation.4 | async-start | bytes 524288 | tf_op jit(solution)/shard_map/all_to_all | solution.py:54
  48.6 15.7 %all_gather.11 = bf16[128,384]{1,0:T(8,128)(2,1)} all-gather(bf16[32,384]{1,0:T(8,128)(2,1)S(1)} %get-tuple-element.4), channel_id=1, replica_groups=mesh['dp'=4,'expert'=4,'loop'=2] {'dp'}, dimensions={0}, use_global_device_ids=true | all-gather | bytes 122880 | tf_op jit(solution)/shard_map/all_gather | solution.py:55
  64.3 0.0 reduce-scatter.2.cloned.1.call-done
  64.3 1.6 %all_to_all.44 = bf16[4,4,4096]{2,1,0:T(4,128)(2,1)} reshape(bf16[16,4096]{1,0:T(8,128)(2,1)} %reduce-scatter.2.cloned.1.call-done) | data formatting | bytes 262144 | tf_op jit(solution)/shard_map/all_to_all | solution.py:53
  66.0 0.0 all-to-all-done.3
  66.0 3.3 %all-to-all-start.2 = ((bf16[4,4,4096]{2,1,0:T(4,128)(2,1)}), bf16[4,4,4096]{2,1,0:T(4,128)(2,1)S(1)}, u32[]{:S(2)}, u32[]{:S(2)}) async-start(bf16[4,4,4096]{2,1,0:T(4,128)(2,1)} %all_to_all.44), calls=%async_computation.3 | async-start | bytes 262144 | tf_op jit(solution)/shard_map/all_to_all | solution.py:53
  69.3 2.4 %convolution_bitcast_fusion = f32[1,1024,384]{2,1,0:T(8,128)} fusion(bf16[128,1024]{1,0:T(8,128)(2,1)S(1)} %bitcast.32, bf16[128,384]{1,0:T(8,128)(2,1)} %all_gather.11), kind=kOutput, calls=%fused_computation.11 | convolution fusion | flops 100663296 | bytes 1933312 | tf_op jit(solution)/shard_map/dot_general | solution.py:56
  71.7 2.1 %all-to-all-done.2 = bf16[4,4,4096]{2,1,0:T(4,128)(2,1)S(1)} async-done(((bf16[4,4,4096]{2,1,0:T(4,128)(2,1)}), bf16[4,4,4096]{2,1,0:T(4,128)(2,1)S(1)}, u32[]{:S(2)}, u32[]{:S(2)}) %all-to-all-start.2) | async-done | bytes 131104 | tf_op jit(solution)/shard_map/all_to_all | solution.py:53
  73.9 0.7 all_to_all.46
  (1 shorter events, 0.0 us)
Async XLA Ops:
  7.2 32.4 %copy-start = (bf16[1,4096,384]{2,1,0:T(8,128)(2,1)S(1)}, bf16[1,4096,384]{2,1,0:T(8,128)(2,1)}, u32[]{:S(2)}) copy-start(bf16[1,4096,384]{2,1,0:T(8,128)(2,1)} %param.10) | copy-start | bytes 9437188
  9.9 8.9 %all-to-all-start = ((bf16[4,4,4096]{2,1,0:T(4,128)(2,1)}), bf16[4,4,4096]{2,1,0:T(4,128)(2,1)S(1)}, u32[]{:S(2)}, u32[]{:S(2)}) async-start(bf16[4,4,4096]{2,1,0:T(4,128)(2,1)} %all_to_all.38), calls=%async_computation | async-start | bytes 262144 | tf_op jit(solution)/shard_map/all_to_all | solution.py:18
  18.8 10.8 %all-to-all-start.1 = ((bf16[4,4,4096]{2,1,0:T(4,128)(2,1)}), bf16[4,4,4096]{2,1,0:T(4,128)(2,1)}, u32[]{:S(2)}, u32[]{:S(2)}) async-start(bf16[4,4,4096]{2,1,0:T(4,128)(2,1)} %all_to_all.41), calls=%async_computation.1 | async-start | bytes 262144 | tf_op jit(solution)/shard_map/all_to_all | solution.py:17
  22.7 41.6 %reduce-scatter.2.cloned.1.call-start = ((), (), s32[]{:S(2)}) async-start(), calls=%async_computation.5 | async-start | bytes 393216 | tf_op jit(solution)/shard_map/reduce_scatter | solution.py:45
  30.5 8.4 %copy-start.1 = (bf16[1,4096,384]{2,1,0:T(8,128)(2,1)S(1)}, bf16[1,4096,384]{2,1,0:T(8,128)(2,1)}, u32[]{:S(2)}) copy-start(bf16[1,4096,384]{2,1,0:T(8,128)(2,1)} %param.9) | copy-start | bytes 9437188
  43.7 22.3 %all-to-all-start.3 = ((bf16[32,4,1024]{2,0,1:T(8,128)(2,1)}), bf16[32,4,1024]{2,0,1:T(8,128)(2,1)S(1)}, u32[]{:S(2)}, u32[]{:S(2)}) async-start(bf16[32,4,1024]{2,0,1:T(8,128)(2,1)} %bitcast.31), calls=%async_computation.4 | async-start | bytes 524288 | tf_op jit(solution)/shard_map/all_to_all | solution.py:54
  66.0 7.9 %all-to-all-start.2 = ((bf16[4,4,4096]{2,1,0:T(4,128)(2,1)}), bf16[4,4,4096]{2,1,0:T(4,128)(2,1)S(1)}, u32[]{:S(2)}, u32[]{:S(2)}) async-start(bf16[4,4,4096]{2,1,0:T(4,128)(2,1)} %all_to_all.44), calls=%async_computation.3 | async-start | bytes 262144 | tf_op jit(solution)/shard_map/all_to_all | solution.py:53
Sparse Core Ops, SparseCore 0:
  43.1 13.1 reduce-scatter.1
where the time goes:
time: 82 us; the launch traced here: 81.4 us
  blocking collectives  28.5 us (35%)
  starting transfers between devices  16.5 us (20%)
  between operations  14.1 us (17%)
  matrix products  8.8 us (11%)
  waiting for transfers between devices  6.05 us (7%)
  local copies, waits for them, and re-layouts  5.53 us (7%)
  other arithmetic  1.94 us (2%)
    all_gather x1, blocking collectives, local(): hidden_all = lax.all_gather(hidden, 'dp', axis=0, tiled=True)  15.7 us
    all_gather x1, blocking collectives, local(): lax.all_gather(arrived_cot, 'loop', axis=0, tiled=True)  6.73 us
    all_gather x1, blocking collectives, local(): lax.all_gather(arrived, 'loop', axis=0, tiled=True)  6 us
    all_to_all x1, starting transfers between devices, local(): lax.all_to_all(gathered_cot, 'dp', split_axis=1, concat_axis=0, tiled=True)  4.9 us
    all_to_all x1, starting transfers between devices, local(): lax.all_to_all(cotans, 'expert', split_axis=0, concat_axis=0, tiled=True)  4.26 us
    all_to_all x1, starting transfers between devices, local(): lax.all_to_all(inputs, 'expert', split_axis=0, concat_axis=0, tiled=True)  3.95 us
    all_to_all x1, waiting for transfers between devices, local(): lax.all_to_all(cotans, 'expert', split_axis=0, concat_axis=0, tiled=True)  3.89 us
    all_to_all x1, starting transfers between devices, local(): lax.all_to_all(summed, 'expert', split_axis=0, concat_axis=0, tiled=True)  3.33 us
  transfers between devices with their start and end apart: 5, of which 2 were waited for; matrix products, arithmetic and copies ran while one was open for 4% of the time, Pallas kernels for 0%

commit v1 on v0

--- a/solution.py
+++ b/solution.py
@@ -2,6 +2,18 @@
 import jax.numpy as jnp
 from jax import lax
 from jax.sharding import PartitionSpec as P
+
+
+def gather_by_bits(x, axis, dim):
+    ways, here = (lax.axis_size(axis), lax.axis_index(axis))
+    grown, reach = (x, 1)
+    while reach < ways:
+        theirs = lax.ppermute(grown, axis, [(d, d ^ reach) for d in range(ways)])
+        mine_first = jnp.concatenate([grown, theirs], axis=dim)
+        theirs_first = jnp.concatenate([theirs, grown], axis=dim)
+        grown = jnp.where(here & reach == 0, mine_first, theirs_first)
+        reach = 2 * reach
+    return grown
 
 
 def local(x_send, cot_send, counts, w_gate, w_up, w_down):
@@ -18,7 +30,7 @@
         lax.all_to_all(cotans, "expert", split_axis=0, concat_axis=0, tiled=True),
     )
     gathered, gathered_cot = (
-        lax.all_gather(arrived, "loop", axis=0, tiled=True),
+        gather_by_bits(arrived, "loop", 0),
         lax.all_gather(arrived_cot, "loop", axis=0, tiled=True),
     )
     gate_local = w_gate[0]

time: 82 us -> 79.5 us (0.970)
  blocking collectives: 28.5 us -> 22.5 us
  starting transfers between devices: 16.5 us -> 18.3 us
  waiting for transfers between devices: 6.05 us -> 7.07 us
    all_gather x1 -> x0, blocking collectives: 6 us -> none  [local(): lax.all_gather(arrived, 'loop', axis=0, tiled=True)]
    ppermute x0 -> x1, starting transfers between devices: none -> 1.81 us  [gather_by_bits(): theirs = lax.ppermute(grown, axis, [(d, d ^ reach) for d in range(ways)])]
    ppermute x0 -> x1, waiting for transfers between devices: none -> 1.02 us  [gather_by_bits(): theirs = lax.ppermute(grown, axis, [(d, d ^ reach) for d in range(ways)])]
  transfers between devices with their start and end apart: 5 -> 6, of which waited for: 2 -> 3; matrix products, arithmetic and copies ran while one was open for 4% -> 7% of each run, Pallas kernels for 0% -> 0%
where the time goes in v1:
time: 79.5 us; the launch traced here: 78.9 us
  blocking collectives  22.5 us (28%)
  starting transfers between devices  18.3 us (23%)
  between operations  14.1 us (18%)
  matrix products  9.45 us (12%)
  waiting for transfers between devices  7.07 us (9%)
  local copies, waits for them, and re-layouts  5.54 us (7%)
  other arithmetic  1.94 us (2%)
    all_gather x1, blocking collectives, local(): hidden_all = lax.all_gather(hidden, 'dp', axis=0, tiled=True)  15.7 us
    all_gather x1, blocking collectives, local(): lax.all_gather(arrived_cot, 'loop', axis=0, tiled=True)  6.72 us
    all_to_all x1, starting transfers between devices, local(): lax.all_to_all(gathered_cot, 'dp', split_axis=1, concat_axis=0, tiled=True)  4.9 us
    all_to_all x1, starting transfers between devices, local(): lax.all_to_all(cotans, 'expert', split_axis=0, concat_axis=0, tiled=True)  4.26 us
    all_to_all x1, starting transfers between devices, local(): lax.all_to_all(inputs, 'expert', split_axis=0, concat_axis=0, tiled=True)  3.95 us
    all_to_all x1, waiting for transfers between devices, local(): lax.all_to_all(cotans, 'expert', split_axis=0, concat_axis=0, tiled=True)  3.89 us
    all_to_all x1, starting transfers between devices, local(): lax.all_to_all(summed, 'expert', split_axis=0, concat_axis=0, tiled=True)  3.33 us
    dot_general x1, matrix products, local(): lax.dot_general(column_part, hidden_all, contract_first, preferred_elemen...  2.43 us
  transfers between devices with their start and end apart: 6, of which 3 were waited for; matrix products, arithmetic and copies ran while one was open for 7% of the time, Pallas kernels for 0%

profile of v1, /device:TPU:0, one launch (start us, length us, event | category | flops | bytes accessed | tf_op | source)
XLA Modules:
  0.0 78.9 jit_solution(11130968878800677489)
XLA Ops:
  7.2 0.0 copy-start
  7.2 0.9 %iota_compare_fusion = pred[4,4]{1,0:T(4,128)(4,1)S(1)} fusion(s32[4]{0:T(128)} %bitcast.31), kind=kLoop, calls=%fused_computation.22 | loop fusion | flops 16 | bytes 32 | tf_op jit(solution)/shard_map/lt | solution.py:22
  8.1 0.1 lt.26
  8.1 1.1 %broadcast_select_fusion.1 = (bf16[16,4096]{1,0:T(8,128)(2,1)S(1)}, bf16[16,4096]{1,0:T(8,128)(2,1)S(1)}) fusion(bf16[16,4096]{1,0:T(8,128)(2,1)} %param.7, pred[16]{0:T(512)(128)(4,1)S(1)} %lt.26, bf16[16,4096]{1,0:T(8,128)(2,1)} %param.6), kind=kLoop, calls=%fused_computation.15 | loop fusion | flops 131072 | bytes 524304 | tf_op jit(solution)/shard_map/jit(_where)/select_n | solution.py:27
  9.2 0.7 all_to_all.38
  9.9 4.3 %all-to-all-start = ((bf16[4,4,4096]{2,1,0:T(4,128)(2,1)}), bf16[4,4,4096]{2,1,0:T(4,128)(2,1)S(1)}, u32[]{:S(2)}, u32[]{:S(2)}) async-start(bf16[4,4,4096]{2,1,0:T(4,128)(2,1)} %all_to_all.38), calls=%async_computation | async-start | bytes 262144 | tf_op jit(solution)/shard_map/all_to_all | solution.py:30
  14.2 0.7 all_to_all.41
  14.9 3.9 %all-to-all-done = bf16[4,4,4096]{2,1,0:T(4,128)(2,1)S(1)} async-done(((bf16[4,4,4096]{2,1,0:T(4,128)(2,1)}), bf16[4,4,4096]{2,1,0:T(4,128)(2,1)S(1)}, u32[]{:S(2)}, u32[]{:S(2)}) %all-to-all-start) | async-done | bytes 131104 | tf_op jit(solution)/shard_map/all_to_all | solution.py:30
  18.8 3.9 %all-to-all-start.1 = ((bf16[4,4,4096]{2,1,0:T(4,128)(2,1)}), bf16[4,4,4096]{2,1,0:T(4,128)(2,1)}, u32[]{:S(2)}, u32[]{:S(2)}) async-start(bf16[4,4,4096]{2,1,0:T(4,128)(2,1)} %all_to_all.41), calls=%async_computation.1 | async-start | bytes 262144 | tf_op jit(solution)/shard_map/all_to_all | solution.py:29
  22.7 0.0 reduce-scatter.2.cloned.1.call-start
  22.8 6.7 %all_gather.6 = bf16[32,4096]{1,0:T(8,128)(2,1)S(1)} all-gather(bf16[16,4096]{1,0:T(8,128)(2,1)S(1)} %all_to_all.40), channel_id=1, replica_groups=mesh['dp'=4,'expert'=4,'loop'=2] {'loop'}, dimensions={0}, use_global_device_ids=true | all-gather | bytes 393216 | tf_op jit(solution)/shard_map/all_gather | solution.py:34
  29.6 0.0 all-to-all-done.1
  29.6 0.9 %all_to_all.43 = bf16[16,4096]{1,0:T(8,128)(2,1)S(1)} reshape(bf16[4,4,4096]{2,1,0:T(4,128)(2,1)} %all-to-all-done.1) | data formatting | bytes 262144 | tf_op jit(solution)/shard_map/all_to_all | solution.py:29
  30.5 0.0 copy-start.1
  30.5 1.8 %collective-permute-start = (bf16[16,4096]{1,0:T(8,128)(2,1)S(1)}, bf16[16,4096]{1,0:T(8,128)(2,1)S(1)}, u32[]{:S(2)}, u32[]{:S(2)}) collective-permute-start(bf16[16,4096]{1,0:T(8,128)(2,1)S(1)} %all_to_all.43), channel_id=1, source_target_pairs={{0,1},{1,0},{2,3},{3,2},{4,5},{5,4},{6,7},{7,6},{8,9},{9,8},{10,11... | collective-permute-start | bytes 393224 | tf_op jit(solution)/shard_map/ppermute | solution.py:11
  32.3 2.4 %fusion.8 = f32[32,384]{1,0:T(8,128)S(1)} fusion(bf16[32,4096]{1,0:T(8,128)(2,1)S(1)} %all_gather.6, bf16[1,4096,384]{2,1,0:T(8,128)(2,1)} %param.11), kind=kOutput, calls=%fused_computation.9 | convolution fusion | flops 100663296 | bytes 3457024 | tf_op jit(solution)/shard_map/dot_general | solution.py:44
  34.8 1.0 %collective-permute-done = bf16[16,4096]{1,0:T(8,128)(2,1)S(1)} collective-permute-done((bf16[16,4096]{1,0:T(8,128)(2,1)S(1)}, bf16[16,4096]{1,0:T(8,128)(2,1)S(1)}, u32[]{:S(2)}, u32[]{:S(2)}) %collective-permute-start) | collective-permute-done | bytes 131104 | tf_op jit(solution)/shard_map/ppermute | solution.py:11
  35.8 0.0 copy-done.1
  35.8 0.6 fusion.3
  36.4 0.0 copy-done
  36.4 1.2 %multiply_convert_fusion = (bf16[32,384]{1,0:T(8,128)(2,1)}, f32[32,384]{1,0:T(8,128)S(1)}) fusion(f32[32,384]{1,0:T(8,128)S(1)} %fusion.3, bf16[1,4096,384]{2,1,0:T(8,128)(2,1)S(1)} %copy-done, bf16[16,4096]{1,0:T(8,128)(2,1)S(1)} %collective-permute-done, bf16[16,4096]{1,0:T(8,128)(2,1)S(1)} %all_to_all.43, pred[]{:T(512)S(6)} %eq.3), kind=kOutput, calls=%fused_computation.16 | convolution fusion | flops 101916672 | bytes 3530753 | tf_op jit(solution)/shard_map/dot_general | solution.py:40
  37.6 1.1 %fusion.1 = f32[32,4096]{1,0:T(8,128)S(1)} fusion(bf16[1,4096,384]{2,1,0:T(8,128)(2,1)S(1)} %copy-done.1, f32[32,384]{1,0:T(8,128)S(1)} %fusion.3, f32[32,384]{1,0:T(8,128)S(1)} %fusion.8, f32[32,384]{1,0:T(8,128)S(1)} %get-tuple-element.5), kind=kOutput, calls=%fused_computation.2 | convolution fusion | flops 100786176 | bytes 3817472 | tf_op jit(solution)/shard_map/dot_general | solution.py:51
  38.6 0.0 copy-start.2
  38.6 1.8 %fusion = bf16[32,4096]{1,0:T(8,128)(2,1)} fusion(f32[32,4096]{1,0:T(8,128)S(1)} %fusion.1, bf16[1,4096,384]{2,1,0:T(8,128)(2,1)S(1)} %copy-done, f32[32,384]{1,0:T(8,128)S(1)} %fusion.8, f32[32,384]{1,0:T(8,128)S(1)} %fusion.3), kind=kOutput, calls=%fused_computation.1 | convolution fusion | flops 100999168 | bytes 4030464 | tf_op jit(solution)/shard_map/dot_general | solution.py:54
  40.4 0.0 reduce-scatter.2.cloned.1.call-update
  40.4 0.7 copy.12
  41.1 4.9 %all-to-all-start.3 = ((bf16[32,4,1024]{2,0,1:T(8,128)(2,1)}), bf16[32,4,1024]{2,0,1:T(8,128)(2,1)S(1)}, u32[]{:S(2)}, u32[]{:S(2)}) async-start(bf16[32,4,1024]{2,0,1:T(8,128)(2,1)} %bitcast.29), calls=%async_computation.4 | async-start | bytes 524288 | tf_op jit(solution)/shard_map/all_to_all | solution.py:66
  46.0 0.0 copy-done.2
  46.1 15.7 %all_gather.7 = bf16[128,384]{1,0:T(8,128)(2,1)} all-gather(bf16[32,384]{1,0:T(8,128)(2,1)S(1)} %copy-done.2), channel_id=1, replica_groups=mesh['dp'=4,'expert'=4,'loop'=2] {'dp'}, dimensions={0}, use_global_device_ids=true | all-gather | bytes 122880 | tf_op jit(solution)/shard_map/all_gather | solution.py:67
  61.8 0.0 reduce-scatter.2.cloned.1.call-done
  61.8 1.6 %all_to_all.44 = bf16[4,4,4096]{2,1,0:T(4,128)(2,1)} reshape(bf16[16,4096]{1,0:T(8,128)(2,1)} %reduce-scatter.2.cloned.1.call-done) | data formatting | bytes 262144 | tf_op jit(solution)/shard_map/all_to_all | solution.py:65
  63.4 0.0 all-to-all-done.3
  63.4 3.3 %all-to-all-start.2 = ((bf16[4,4,4096]{2,1,0:T(4,128)(2,1)}), bf16[4,4,4096]{2,1,0:T(4,128)(2,1)S(1)}, u32[]{:S(2)}, u32[]{:S(2)}) async-start(bf16[4,4,4096]{2,1,0:T(4,128)(2,1)} %all_to_all.44), calls=%async_computation.3 | async-start | bytes 262144 | tf_op jit(solution)/shard_map/all_to_all | solution.py:65
  66.8 2.4 %convolution_bitcast_fusion = f32[1,1024,384]{2,1,0:T(8,128)} fusion(bf16[128,1024]{1,0:T(8,128)(2,1)S(1)} %bitcast.30, bf16[128,384]{1,0:T(8,128)(2,1)} %all_gather.7), kind=kOutput, calls=%fused_computation.11 | convolution fusion | flops 100663296 | bytes 1933312 | tf_op jit(solution)/shard_map/dot_general | solution.py:68
  69.2 2.1 %all-to-all-done.2 = bf16[4,4,4096]{2,1,0:T(4,128)(2,1)S(1)} async-done(((bf16[4,4,4096]{2,1,0:T(4,128)(2,1)}), bf16[4,4,4096]{2,1,0:T(4,128)(2,1)S(1)}, u32[]{:S(2)}, u32[]{:S(2)}) %all-to-all-start.2) | async-done | bytes 131104 | tf_op jit(solution)/shard_map/all_to_all | solution.py:65
  71.3 0.7 all_to_all.46
  (1 shorter events, 0.0 us)
Async XLA Ops:
  7.2 29.2 %copy-start = (bf16[1,4096,384]{2,1,0:T(8,128)(2,1)S(1)}, bf16[1,4096,384]{2,1,0:T(8,128)(2,1)}, u32[]{:S(2)}) copy-start(bf16[1,4096,384]{2,1,0:T(8,128)(2,1)} %param.10) | copy-start | bytes 9437188
  9.9 8.9 %all-to-all-start = ((bf16[4,4,4096]{2,1,0:T(4,128)(2,1)}), bf16[4,4,4096]{2,1,0:T(4,128)(2,1)S(1)}, u32[]{:S(2)}, u32[]{:S(2)}) async-start(bf16[4,4,4096]{2,1,0:T(4,128)(2,1)} %all_to_all.38), calls=%async_computation | async-start | bytes 262144 | tf_op jit(solution)/shard_map/all_to_all | solution.py:30
  18.8 10.8 %all-to-all-start.1 = ((bf16[4,4,4096]{2,1,0:T(4,128)(2,1)}), bf16[4,4,4096]{2,1,0:T(4,128)(2,1)}, u32[]{:S(2)}, u32[]{:S(2)}) async-start(bf16[4,4,4096]{2,1,0:T(4,128)(2,1)} %all_to_all.41), calls=%async_computation.1 | async-start | bytes 262144 | tf_op jit(solution)/shard_map/all_to_all | solution.py:29
  22.7 39.1 %reduce-scatter.2.cloned.1.call-start = ((), (), s32[]{:S(2)}) async-start(), calls=%async_computation.5 | async-start | bytes 393216 | tf_op jit(solution)/shard_map/reduce_scatter | solution.py:57
  30.5 5.3 %copy-start.1 = (bf16[1,4096,384]{2,1,0:T(8,128)(2,1)S(1)}, bf16[1,4096,384]{2,1,0:T(8,128)(2,1)}, u32[]{:S(2)}) copy-start(bf16[1,4096,384]{2,1,0:T(8,128)(2,1)} %param.9) | copy-start | bytes 9437188
  30.5 5.3 %collective-permute-start = (bf16[16,4096]{1,0:T(8,128)(2,1)S(1)}, bf16[16,4096]{1,0:T(8,128)(2,1)S(1)}, u32[]{:S(2)}, u32[]{:S(2)}) collective-permute-start(bf16[16,4096]{1,0:T(8,128)(2,1)S(1)} %all_to_all.43), channel_id=1, source_target_pairs={{0,1},{1,0},{2,3},{3,2},{4,5},{5,4},{6,7},{7,6},{8,9},{9,8},{10,11... | collective-permute-start | bytes 393224 | tf_op jit(solution)/shard_map/ppermute | solution.py:11
  38.6 7.4 %copy-start.2 = (bf16[32,384]{1,0:T(8,128)(2,1)S(1)}, bf16[32,384]{1,0:T(8,128)(2,1)}, u32[]{:S(2)}) copy-start(bf16[32,384]{1,0:T(8,128)(2,1)} %get-tuple-element.4) | copy-start | bytes 73732
  41.1 22.3 %all-to-all-start.3 = ((bf16[32,4,1024]{2,0,1:T(8,128)(2,1)}), bf16[32,4,1024]{2,0,1:T(8,128)(2,1)S(1)}, u32[]{:S(2)}, u32[]{:S(2)}) async-start(bf16[32,4,1024]{2,0,1:T(8,128)(2,1)} %bitcast.29), calls=%async_computation.4 | async-start | bytes 524288 | tf_op jit(solution)/shard_map/all_to_all | solution.py:66
  63.4 7.9 %all-to-all-start.2 = ((bf16[4,4,4096]{2,1,0:T(4,128)(2,1)}), bf16[4,4,4096]{2,1,0:T(4,128)(2,1)S(1)}, u32[]{:S(2)}, u32[]{:S(2)}) async-start(bf16[4,4,4096]{2,1,0:T(4,128)(2,1)} %all_to_all.44), calls=%async_computation.3 | async-start | bytes 262144 | tf_op jit(solution)/shard_map/all_to_all | solution.py:65
Sparse Core Ops, SparseCore 0:
  40.5 13.1 reduce-scatter.1
